TPU v7x, 256 devices: a whole 4x4x8 slice. The times are simulated.
256 devices in a mesh: tm: 32 (over y, z), space: 8 (over x, core).
Axes of the slice: x: 4, y: 4, z: 8, core: 2. Of those that a mesh axis runs over, the one named last changes fastest.
Arguments:
- inverse_factor: bfloat16 [2, 32, 4096, 4096], P(None, 'tm', 'space'), may hold values from -1.5 to 1.5, as said below
- tile_mask: int32 [32, 32], replicated, may hold values 0 or 1
- carry_rate: float32 [32, 4096, 2], P('tm', 'space'), may hold values from 0 to 1
- right_side: float32 [32, 4096, 2, 128], P('tm', 'space'), may hold values from -1.5 to 1.5
- arrow_rows: bfloat16 [32, 4096, 2, 512], P('tm', 'space'), may hold values from -0.0625 to 0.0625
- fixed_rhs: float32 [2, 512, 128], P(None, ('tm', 'space')), may hold values from -6 to 6
- tip_factor: bfloat16 [2, 512, 512], replicated, may hold values from -1 to 1, as said below
Outputs:
- solution: float32 [32, 4096, 2, 128], P('tm', 'space')
- fixed_solution: float32 [2, 512, 128], P(None, ('tm', 'space'))
Inputs may be any that keep to these rules, and one draw needn't show every extreme that they name: `tile_mask`: 1 marks a tile that may be nonzero. `inverse_factor`: only entries on or below the diagonal are read. `tip_factor`: only entries on or below the diagonal are read.
All inputs are finite; a program needn't handle non-finite values.
Results may differ from a plain program's by a relative error of at most 0.022.
Values may be sent and summed in bfloat16 or wider, within the bound.
No kernel may reach another device: no remote copies, remote signals or barrier semaphores. Data moves between devices by JAX's collectives and lax.ppermute only.
A program may use at most 320 MiB of HBM per device.

v0:
```python
import jax
import jax.numpy as jnp
from jax import lax
from jax.sharding import PartitionSpec as P

TILE = 128


def carried_in(shard, axis, join, neutral, backward):
    count = lax.axis_size(axis)
    place = lax.axis_index(axis)
    ahead = count - 1 - place if backward else place
    gathered = jax.tree.map(
        lambda a, kind: lax.all_gather(a.astype(kind), axis), shard, (jnp.bfloat16, jnp.bfloat16)
    )
    state = jax.tree.map(lambda a, e: jnp.zeros_like(a) + jnp.asarray(e, a.dtype), shard, neutral)

    def one(turn, state):
        source = count - 1 - turn if backward else turn
        return join(
            state,
            jax.tree.map(
                lambda a, own: lax.dynamic_index_in_dim(a, source, 0, False).astype(own.dtype),
                gathered,
                shard,
            ),
        )

    return lax.fori_loop(0, ahead, one, state)


def combine(earlier, latter):
    rate_new = latter[0] * earlier[0]
    rest = tuple(
        (value_l + latter[0] * value_e for value_l, value_e in zip(latter[1:], earlier[1:]))
    )
    return (rate_new,) + rest


def tile_keep(tile_table, row_start, row_total, col_total):
    tile_count = tile_table.shape[0]
    tile_ids = jnp.arange(tile_count, dtype=jnp.int32)
    row_index = row_start + jnp.arange(row_total, dtype=jnp.int32)
    col_index = jnp.arange(col_total, dtype=jnp.int32)
    row_onehot = (row_index[:, None] // TILE == tile_ids[None, :]).astype(jnp.float32)
    col_onehot = (col_index[:, None] // TILE == tile_ids[None, :]).astype(jnp.float32)
    marked = jnp.dot(jnp.dot(row_onehot, tile_table.astype(jnp.float32)), col_onehot.T)
    return (marked > 0.5) & (row_index[:, None] >= col_index[None, :])


def on_device(inverse_factor, tile_mask, carry_rate, right_side, arrow_rows, fixed_rhs, tip_factor):
    row_count = right_side.shape[1]
    node_total = inverse_factor.shape[3]
    row_start = lax.axis_index("space") * row_count
    tile_table = jnp.maximum(tile_mask, jnp.eye(tile_mask.shape[0], dtype=jnp.int32))
    weights = inverse_factor[:, 0]
    bf_zero = jnp.zeros((), jnp.bfloat16)
    rate_col = carry_rate[0][:, :, None]
    source = right_side[0]
    unit_rate = jnp.ones_like(rate_col)
    earlier_sum = carried_in(
        (rate_col, source), "tm", combine, (unit_rate, jnp.zeros_like(source)), False
    )
    forward = source + rate_col * earlier_sum[1]
    forward_b = forward.astype(jnp.bfloat16)
    row_keep = tile_keep(tile_table, row_start, row_count, node_total)
    masked_rows = jnp.where(row_keep[None], weights, bf_zero)
    block = masked_rows
    inner_rows = jnp.einsum(
        "hrn,nhk->rhk",
        block,
        lax.all_gather(forward_b, "space", axis=0, tiled=True),
        preferred_element_type=jnp.float32,
    ).astype(jnp.bfloat16)
    block = masked_rows
    scaled = lax.psum_scatter(
        jnp.einsum("hrn,rhk->nhk", block, inner_rows, preferred_element_type=jnp.float32).astype(
            jnp.bfloat16
        ),
        "space",
        scatter_dimension=0,
        tiled=True,
    ).astype(jnp.float32)
    arrow_part = arrow_rows[0]
    coupling = jnp.einsum("rhf,rhk->hfk", arrow_part, forward_b, preferred_element_type=jnp.float32)
    share_rows = fixed_rhs.shape[1]
    share_start = lax.axis_index(("tm", "space")) * share_rows
    contrib = -coupling
    own_part = lax.dynamic_slice_in_dim(contrib, share_start, share_rows, 1) + fixed_rhs
    contrib = lax.dynamic_update_slice_in_dim(contrib, own_part, share_start, 1)
    fixed_forward = lax.psum(contrib, ("tm", "space")).astype(jnp.bfloat16)
    fixed_total = tip_factor.shape[1]
    fixed_index = jnp.arange(fixed_total, dtype=jnp.int32)
    lower_tri = fixed_index[:, None] >= fixed_index[None, :]
    tip_lower = jnp.where(lower_tri[None], tip_factor, bf_zero)
    tip_inner = jnp.einsum(
        "hij,hjk->hik", tip_lower, fixed_forward, preferred_element_type=jnp.float32
    ).astype(jnp.bfloat16)
    fixed_solution = jnp.einsum(
        "hij,hik->hjk", tip_lower, tip_inner, preferred_element_type=jnp.float32
    )
    fixed_own = lax.dynamic_slice_in_dim(fixed_solution, share_start, share_rows, 1)
    fixed_b = fixed_solution.astype(jnp.bfloat16)
    carried = scaled - jnp.einsum(
        "rhf,hfk->rhk", arrow_part, fixed_b, preferred_element_type=jnp.float32
    )
    following = carried_in(
        (rate_col, rate_col * carried), "tm", combine, (unit_rate, jnp.zeros_like(carried)), True
    )
    solution = carried + following[1]
    return (solution[None], fixed_own)


def solution(mesh):
    placed = (
        P(None, "tm", "space", None),
        P(),
        P("tm", "space", None),
        P("tm", "space", None, None),
        P("tm", "space", None, None),
        P(None, ("tm", "space"), None),
        P(),
    )
    return jax.shard_map(
        on_device,
        mesh=mesh,
        in_specs=placed,
        out_specs=(P("tm", "space", None, None), P(None, ("tm", "space"), None)),
        check_vma=False,
    )
```

profile of v0, /device:TPU:2, one launch (start us, length us, event | category | flops | bytes accessed | tf_op | source)
XLA Modules:
  0.0 596.0 jit_solution(12626880782622736189)
XLA Ops:
  7.2 1.9 copy.62
  9.2 1.2 copy.34
  11.1 52.1 %all-gather = bf16[32,512,2]{1,2,0:T(2,128)(2,1)S(1)} all-gather(bf16[1,512,2]{1,2,0:T(2,128)(2,1)S(1)} %convert_element_type.103), channel_id=2, replica_groups=mesh['tm'=32,'space'=8] {'tm'}, dimensions={0}, use_global_device_ids=true | all-gather | bytes 67584 | tf_op jit(solution)/shard_map/all_gather | solution.py:14
  63.2 3.3 copy.37
  66.6 46.1 %all-gather.6.cloned.1.call-done = bf16[32,512,2,128]{3,1,2,0:T(8,128)(2,1)} async-done(((bf16[1,512,2,128]{3,1,2,0:T(8,128)(2,1)}), bf16[32,512,2,128]{3,1,2,0:T(8,128)(2,1)}) %all-gather.6.cloned.1.call-update) | async-done | bytes 8388624 | tf_op jit(solution)/shard_map/all_gather | solution.py:14
  114.4 4.2 fusion
  118.6 154.2 %all-gather.8.cloned.1.call-done = bf16[4096,2,128]{0,2,1:T(8,128)(2,1)} async-done(((bf16[512,2,128]{0,2,1:T(8,128)(2,1)}), bf16[4096,2,128]{0,2,1:T(8,128)(2,1)}) %all-gather.8.cloned.1.call-update) | async-done | bytes 2097168 | tf_op jit(solution)/shard_map/all_gather | solution.py:72
  272.7 13.2 %fusion.4 = bf16[4096,2,128]{0,2,1:T(8,128)(2,1)} fusion(bf16[2,1,512,4096]{3,2,1,0:T(8,128)(2,1)} %param.11, pred[512,4096]{1,0:T(8,128)(4,1)} %fusion, bf16[4096,2,128]{0,2,1:T(8,128)(2,1)} %all-gather.8.cloned.1.call-done), kind=kOutput, calls=%fused_computation.12 | convolution fusion | flops 2157051904 | bytes 14680064 | tf_op jit(solution)/shard_map/hrn,rhk->nhk/dot_general | solution.py:77
  286.7 1.1 dynamic_update_slice.3
  287.8 78.9 %all-reduce.1 = bf16[2,512,128]{1,2,0:T(8,128)(2,1)S(1)} all-reduce(f32[2,512,128]{1,2,0:T(8,128)S(1)} %dynamic_update_slice.3), channel_id=1, replica_groups=mesh['tm'=32,'space'=8] {'tm','space'}, use_global_device_ids=true, to_apply=%region_3.4 | all-reduce | flops 131072 | bytes 786432 | tf_op jit(solution)/shard_map/psum | solution.py:91
  366.7 2.3 fusion.9
  369.0 2.1 multiply_convert_fusion
  371.8 102.9 %all-gather.10.cloned.1.call-done = bf16[16384,2,128]{0,2,1:T(8,128)(2,1)} async-done(((bf16[512,2,128]{0,2,1:T(8,128)(2,1)}), bf16[16384,2,128]{0,2,1:T(8,128)(2,1)}) %all-gather.10.cloned.1.call-update) | async-done | bytes 8388624 | tf_op jit(solution)/shard_map/all_gather | solution.py:14
  474.7 21.1 %copy.52 = bf16[16384,2,128]{2,1,0:T(2,128)(2,1)} copy(bf16[16384,2,128]{0,2,1:T(8,128)(2,1)} %all-gather.10.cloned.1.call-done) | data formatting | bytes 16777216 | tf_op jit(solution)/shard_map/while | solution.py:29
  495.9 92.2 %while.27 = (s32[]{:T(128)}, f32[512,2,128]{2,1,0:T(2,128)S(1)}, s32[]{:T(128)}, bf16[32,512,2,128]{3,2,1,0:T(2,128)(2,1)}, bf16[32,512,2,1]{2,1,3,0:T(8,128)(2,...) while((s32[]{:T(128)}, f32[512,2,128]{2,1,0:T(2,128)S(1)}, s32[]{:T(128)}, ...), condition=%wide.region_5.6_spmd, body=%wide.region_4.5_spmd.sunk | while | flops 394246 | bytes 1321107 | solution.py:29
  495.9 0.9 bitcast_convert_fusion.5
  496.9 2.0 convert_add_fusion.5
  499.8 2.0 convert_add_fusion.5
  502.8 2.0 convert_add_fusion.5
  505.8 2.0 convert_add_fusion.5
  508.8 2.0 convert_add_fusion.5
  511.7 2.0 convert_add_fusion.5
  514.7 2.0 convert_add_fusion.5
  517.7 2.0 convert_add_fusion.5
  520.7 2.0 convert_add_fusion.5
  523.6 2.0 convert_add_fusion.5
  526.6 2.0 convert_add_fusion.5
  529.6 2.0 convert_add_fusion.5
  532.6 2.0 convert_add_fusion.5
  535.5 2.0 convert_add_fusion.5
  538.5 2.0 convert_add_fusion.5
  541.5 2.0 convert_add_fusion.5
  544.5 2.0 convert_add_fusion.5
  547.4 2.0 convert_add_fusion.5
  550.4 2.0 convert_add_fusion.5
  553.4 2.0 convert_add_fusion.5
  556.3 2.0 convert_add_fusion.5
  559.3 2.0 convert_add_fusion.5
  562.3 2.0 convert_add_fusion.5
  565.3 2.0 convert_add_fusion.5
  568.2 2.0 convert_add_fusion.5
  571.2 2.0 convert_add_fusion.5
  574.2 2.0 convert_add_fusion.5
  577.2 2.0 convert_add_fusion.5
  580.1 2.0 convert_add_fusion.5
  583.1 2.0 convert_add_fusion.5
  586.1 2.0 convert_add_fusion.5
  588.4 1.0 copy.48
  (64 shorter events, 32.1 us)
Async XLA Ops:
  7.2 279.1 %copy-start = (bf16[1,512,2,512]{3,2,1,0:T(2,128)(2,1)S(1)}, bf16[1,512,2,512]{3,2,1,0:T(2,128)(2,1)}, u32[]{:S(2)}) copy-start(bf16[1,512,2,512]{3,2,1,0:T(2,128)(2,1)} %param.15) | copy-start | bytes 3145732
  7.2 105.5 %all-gather.6.cloned.1.call-start = ((), (), s32[]{:S(2)}) async-start(), calls=%async_computation.1 | async-start | bytes 8650752 | tf_op jit(solution)/shard_map/all_gather | solution.py:14
  9.1 263.6 %all-gather.8.cloned.1.call-start = ((), (), s32[]{:S(2)}) async-start(), calls=%async_computation.2 | async-start | bytes 2359296 | tf_op jit(solution)/shard_map/all_gather | solution.py:72
  112.8 0.7 copy-start.2
  112.8 1.6 copy-start.4
  114.3 254.7 %reduce-scatter.2.cloned.1.call-start = ((), (), s32[]{:S(2)}) async-start(), calls=%async_computation.3 | async-start | bytes 2359296 | tf_op jit(solution)/shard_map/reduce_scatter | solution.py:76
  118.6 167.5 %copy-start.3 = (f32[2,2,128]{2,1,0:T(2,128)S(1)}, f32[2,2,128]{2,1,0:T(2,128)}, u32[]{:S(2)}) copy-start(f32[2,2,128]{2,1,0:T(2,128)} %param.16) | copy-start | bytes 6148
  118.6 167.7 %copy-start.1 = (bf16[512,2,128]{0,2,1:T(8,128)(2,1)S(1)}, bf16[512,2,128]{0,2,1:T(8,128)(2,1)}, u32[]{:S(2)}) copy-start(bf16[512,2,128]{0,2,1:T(8,128)(2,1)} %fusion.19) | copy-start | bytes 786436
  286.0 188.7 %all-gather.10.cloned.1.call-start = ((), (), s32[]{:S(2)}) async-start(), calls=%async_computation.4 | async-start | bytes 8650752 | tf_op jit(solution)/shard_map/all_gather | solution.py:14
Sparse Core Ops, SparseCore 0:
  11.2 101.4 all-gather.5
  115.0 157.6 all-gather.7
  286.1 34.6 reduce-scatter.1
  371.3 103.2 all-gather.9
where the time goes:
time: 598 us; the launch traced here: 596 us
  waiting for transfers between devices  303 us (51%)
  blocking collectives  131 us (22%)
  other arithmetic  92.9 us (16%)
  local copies, waits for them, and re-layouts  31.4 us (5%)
  matrix products  22.2 us (4%)
  between operations  14 us (2%)
    all_gather x1, waiting for transfers between devices, on_device(): lax.all_gather(forward_b, 'space', axis=0, tiled=True)  154 us
    all_gather x2, waiting for transfers between devices, carried_in(): lax.all_gather(a.astype(kind), axis)  149 us
    psum x1, blocking collectives, on_device(): fixed_forward = lax.psum(contrib, ('tm', 'space')).astype(jnp.bfloat16)  78.9 us
    add x31, other arithmetic, combine(): value_l + latter[0] * value_e  62.3 us
    all_gather x1, blocking collectives, carried_in(): lax.all_gather(a.astype(kind), axis)  52.1 us
    convert_element_type x31, other arithmetic, one(): lax.dynamic_index_in_dim(a, source, 0, False).astype(own.dtype)  28.8 us
    while x4, local copies, waits for them, and re-layouts, carried_in(): return lax.fori_loop(0, ahead, one, state)  24.8 us
    dot_general x1, matrix products, on_device(): jnp.einsum('hrn,rhk->nhk', block, inner_rows, preferred_element_type=jnp....  13.2 us
  transfers between devices with their start and end apart: 4, of which 3 were waited for; matrix products, arithmetic and copies ran while one was open for 2% of the time, Pallas kernels for 0%

commit v1 on v0

--- a/solution.py
+++ b/solution.py
@@ -4,6 +4,22 @@
 from jax.sharding import PartitionSpec as P
 
 TILE = 128
+
+
+def summed_both_ways(x, axis, dim, term):
+    peers, position, rows = (lax.axis_size(axis), lax.axis_index(axis), x.shape[dim])
+    right = [(i, (i + 1) % peers) for i in range(peers)]
+    left = [(i, (i - 1) % peers) for i in range(peers)]
+    half = peers // 2
+    from_left = from_right = x
+    subtotal = term(x, position * rows)
+    for hop in range(1, half + 1):
+        from_left = lax.ppermute(from_left, axis, right)
+        if hop < peers - half:
+            from_right = lax.ppermute(from_right, axis, left)
+            subtotal = subtotal + term(from_right, (position + hop) % peers * rows)
+        subtotal = subtotal + term(from_left, (position - hop) % peers * rows)
+    return subtotal
 
 
 def carried_in(shard, axis, join, neutral, backward):
@@ -66,11 +82,16 @@
     row_keep = tile_keep(tile_table, row_start, row_count, node_total)
     masked_rows = jnp.where(row_keep[None], weights, bf_zero)
     block = masked_rows
-    inner_rows = jnp.einsum(
-        "hrn,nhk->rhk",
-        block,
-        lax.all_gather(forward_b, "space", axis=0, tiled=True),
-        preferred_element_type=jnp.float32,
+    inner_rows = summed_both_ways(
+        forward_b,
+        "space",
+        0,
+        lambda shard_2, start: jnp.einsum(
+            "hrn,nhk->rhk",
+            lax.dynamic_slice_in_dim(block, start, shard_2.shape[0], axis=2),
+            shard_2,
+            preferred_element_type=jnp.float32,
+        ),
     ).astype(jnp.bfloat16)
     block = masked_rows
     scaled = lax.psum_scatter(

time: 598 us -> 596 us (level)
  waiting for transfers between devices: 303 us -> 147 us
  blocking collectives: 131 us -> 266 us
  other arithmetic: 92.9 us -> 101 us
    all_gather x1 -> x0, waiting for transfers between devices: 154 us -> none  [on_device(): lax.all_gather(forward_b, 'space', axis=0, tiled=True)]
    psum x1, blocking collectives: 78.9 us -> 214 us  [on_device(): fixed_forward = lax.psum(contrib, ('tm', 'space')).astype(jnp.bfloat16)]
    dot_general x0 -> x7, matrix products: none -> 11.9 us  [on_device(): jnp.einsum('hrn,nhk->rhk', lax.dynamic_slice_in_dim(block, start, shard_2...]
    select_n x0 -> x1, other arithmetic: none -> 8.49 us  [on_device(): masked_rows = jnp.where(row_keep[None], weights, bf_zero)]
    dot_general x1, matrix products: 13.2 us -> 6.71 us  [on_device(): jnp.einsum('hrn,rhk->nhk', block, inner_rows, preferred_element_type=jnp....]
  transfers between devices with their start and end apart: 4 -> 10, of which waited for: 3 -> 5; matrix products, arithmetic and copies ran while one was open for 2% -> 6% of each run, Pallas kernels for 0% -> 0%
where the time goes in v1:
time: 596 us; the launch traced here: 593 us
  blocking collectives  266 us (45%)
  waiting for transfers between devices  147 us (25%)
  other arithmetic  101 us (17%)
  local copies, waits for them, and re-layouts  31 us (5%)
  matrix products  28 us (5%)
  between operations  14 us (2%)
    psum x1, blocking collectives, on_device(): fixed_forward = lax.psum(contrib, ('tm', 'space')).astype(jnp.bfloat16)  214 us
    all_gather x2, waiting for transfers between devices, carried_in(): lax.all_gather(a.astype(kind), axis)  143 us
    add x31, other arithmetic, combine(): value_l + latter[0] * value_e  62.3 us
    all_gather x1, blocking collectives, carried_in(): lax.all_gather(a.astype(kind), axis)  52.1 us
    convert_element_type x31, other arithmetic, one(): lax.dynamic_index_in_dim(a, source, 0, False).astype(own.dtype)  28.7 us
    while x4, local copies, waits for them, and re-layouts, carried_in(): return lax.fori_loop(0, ahead, one, state)  24.8 us
  transfers between devices with their start and end apart: 10, of which 5 were waited for; matrix products, arithmetic and copies ran while one was open for 6% of the time, Pallas kernels for 0%

profile of v1, /device:TPU:2, one launch (start us, length us, event | category | flops | bytes accessed | tf_op | source)
XLA Modules:
  0.0 593.4 jit_solution(5634916871451262593)
XLA Ops:
  7.2 1.9 copy.62
  11.1 52.1 %all-gather = bf16[32,512,2]{1,2,0:T(2,128)(2,1)S(1)} all-gather(bf16[1,512,2]{1,2,0:T(2,128)(2,1)S(1)} %convert_element_type.100), channel_id=2, replica_groups=mesh['tm'=32,'space'=8] {'tm'}, dimensions={0}, use_global_device_ids=true | all-gather | bytes 67584 | tf_op jit(solution)/shard_map/all_gather | solution.py:30
  63.2 3.3 copy.37
  66.6 4.6 fusion
  71.2 41.4 %all-gather.5.cloned.1.call-done = bf16[32,512,2,128]{3,1,2,0:T(8,128)(2,1)} async-done(((bf16[1,512,2,128]{3,1,2,0:T(8,128)(2,1)}), bf16[32,512,2,128]{3,1,2,0:T(8,128)(2,1)}) %all-gather.5.cloned.1.call-update) | async-done | bytes 8388624 | tf_op jit(solution)/shard_map/all_gather | solution.py:30
  113.2 1.7 collective-permute-start
  114.9 8.5 %bitcast_select_fusion = bf16[2,512,4096]{2,1,0:T(8,128)(2,1)} fusion(bf16[2,1,512,4096]{3,2,1,0:T(8,128)(2,1)} %param.11, pred[512,4096]{1,0:T(8,128)(4,1)} %fusion), kind=kLoop, calls=%fused_computation.6 | loop fusion | flops 4194304 | bytes 18874368 | tf_op jit(solution)/shard_map/jit(_where)/select_n | solution.py:83
  125.1 1.7 collective-permute-start.2
  130.9 2.0 collective-permute-start.4
  140.1 2.4 collective-permute-done.6
  142.5 6.7 %fusion.1 = bf16[4096,2,128]{0,2,1:T(8,128)(2,1)} fusion(bf16[2,512,4096]{2,1,0:T(8,128)(2,1)} %bitcast_select_fusion, f32[2,128,512]{2,1,0:T(8,128)S(1)} %fusion.3, bf16[512,2,128]{0,2,1:T(8,128)(2,1)S(1)} %collective-permute-done.6, s32[]{:T(128)S(6)} %select_n.122), kind=kOutput, calls=%fused_computation.10 | convolution fusion | flops 1209270272 | bytes 12320772 | tf_op jit(solution)/shard_map/hrn,rhk->nhk/dot_general | solution.py:98
  151.0 214.3 %all-reduce.1 = bf16[2,512,128]{1,2,0:T(8,128)(2,1)S(1)} all-reduce(f32[2,512,128]{1,2,0:T(8,128)S(1)} %dynamic_update_slice.3), channel_id=1, replica_groups=mesh['tm'=32,'space'=8] {'tm','space'}, use_global_device_ids=true, to_apply=%region_3.4 | all-reduce | flops 131072 | bytes 786432 | tf_op jit(solution)/shard_map/psum | solution.py:112
  365.3 2.3 fusion.6
  367.7 2.1 multiply_convert_fusion
  370.4 101.9 %all-gather.7.cloned.1.call-done = bf16[16384,2,128]{0,2,1:T(8,128)(2,1)} async-done(((bf16[512,2,128]{0,2,1:T(8,128)(2,1)}), bf16[16384,2,128]{0,2,1:T(8,128)(2,1)}) %all-gather.7.cloned.1.call-update) | async-done | bytes 8388624 | tf_op jit(solution)/shard_map/all_gather | solution.py:30
  472.3 21.1 %copy.52 = bf16[16384,2,128]{2,1,0:T(2,128)(2,1)} copy(bf16[16384,2,128]{0,2,1:T(8,128)(2,1)} %all-gather.7.cloned.1.call-done) | data formatting | bytes 16777216 | tf_op jit(solution)/shard_map/while | solution.py:45
  493.5 92.0 %while.27 = (s32[]{:T(128)}, f32[512,2,128]{2,1,0:T(2,128)S(1)}, s32[]{:T(128)}, bf16[32,512,2,128]{3,2,1,0:T(2,128)(2,1)}, bf16[32,512,2,1]{2,1,3,0:T(8,128)(2,...) while((s32[]{:T(128)}, f32[512,2,128]{2,1,0:T(2,128)S(1)}, s32[]{:T(128)}, ...), condition=%wide.region_5.6_spmd, body=%wide.region_4.5_spmd.sunk | while | flops 394246 | bytes 1321115 | solution.py:45
  494.5 2.0 convert_add_fusion.5
  497.4 2.0 convert_add_fusion.5
  500.4 2.0 convert_add_fusion.5
  503.4 2.0 convert_add_fusion.5
  506.4 2.0 convert_add_fusion.5
  509.3 2.0 convert_add_fusion.5
  512.3 2.0 convert_add_fusion.5
  515.3 2.0 convert_add_fusion.5
  518.2 2.0 convert_add_fusion.5
  521.2 2.0 convert_add_fusion.5
  524.2 2.0 convert_add_fusion.5
  527.1 2.0 convert_add_fusion.5
  530.1 2.0 convert_add_fusion.5
  533.1 2.0 convert_add_fusion.5
  536.0 2.0 convert_add_fusion.5
  539.0 2.0 convert_add_fusion.5
  542.0 2.0 convert_add_fusion.5
  544.9 2.0 convert_add_fusion.5
  547.9 2.0 convert_add_fusion.5
  550.9 2.0 convert_add_fusion.5
  553.9 2.0 convert_add_fusion.5
  556.8 2.0 convert_add_fusion.5
  559.8 2.0 convert_add_fusion.5
  562.8 2.0 convert_add_fusion.5
  565.7 2.0 convert_add_fusion.5
  568.7 2.0 convert_add_fusion.5
  571.7 2.0 convert_add_fusion.5
  574.6 2.0 convert_add_fusion.5
  577.6 2.0 convert_add_fusion.5
  580.6 2.0 convert_add_fusion.5
  583.5 2.0 convert_add_fusion.5
  (79 shorter events, 48.0 us)
Async XLA Ops:
  7.2 142.4 %copy-start = (bf16[1,512,2,512]{3,2,1,0:T(2,128)(2,1)S(1)}, bf16[1,512,2,512]{3,2,1,0:T(2,128)(2,1)}, u32[]{:S(2)}) copy-start(bf16[1,512,2,512]{3,2,1,0:T(2,128)(2,1)} %param.15) | copy-start | bytes 3145732
  7.2 105.5 %all-gather.5.cloned.1.call-start = ((), (), s32[]{:S(2)}) async-start(), calls=%async_computation.1 | async-start | bytes 8650752 | tf_op jit(solution)/shard_map/all_gather | solution.py:30
  9.1 358.5 %reduce-scatter.2.cloned.1.call-start = ((), (), s32[]{:S(2)}) async-start(), calls=%async_computation.2 | async-start | bytes 2359296 | tf_op jit(solution)/shard_map/reduce_scatter | solution.py:97
  71.2 41.8 %copy-start.1 = (f32[1,512,2]{1,2,0:T(2,128)S(1)}, f32[1,512,2]{1,2,0:T(2,128)}, u32[]{:S(2)}) copy-start(f32[1,512,2]{1,2,0:T(2,128)} %param.13) | copy-start | bytes 12292
  113.1 11.9 %collective-permute-start.1 = (bf16[512,2,128]{0,2,1:T(8,128)(2,1)S(1)}, bf16[512,2,128]{0,2,1:T(8,128)(2,1)S(1)}, u32[]{:S(2)}, u32[]{:S(2)}) collective-permute-start(bf16[512,2,128]{0,2,1:T(8,128)(2,1)S(1)} %fusion.28), channel_id=1, source_target_pairs={{0,1},{1,2},{2,3},{3,4},{4,5},{5,6},{6,7},{7,0},{8,9},{9,10},{10,1... | collective-permute-start | bytes 786440 | tf_op jit(solution)/shard_map/ppermute | solution.py:17
  113.2 12.0 %collective-permute-start = (bf16[512,2,128]{0,2,1:T(8,128)(2,1)S(1)}, bf16[512,2,128]{0,2,1:T(8,128)(2,1)S(1)}, u32[]{:S(2)}, u32[]{:S(2)}) collective-permute-start(bf16[512,2,128]{0,2,1:T(8,128)(2,1)S(1)} %fusion.28), channel_id=1, source_target_pairs={{0,7},{1,0},{2,1},{3,2},{4,3},{5,4},{6,5},{7,6},{8,15},{9,8},{10,9... | collective-permute-start | bytes 786440 | tf_op jit(solution)/shard_map/ppermute | solution.py:19
  125.1 5.8 collective-permute-start.3
  125.1 5.8 collective-permute-start.2
  130.9 5.8 collective-permute-start.5
  130.9 7.5 %collective-permute-start.4 = (bf16[512,2,128]{0,2,1:T(8,128)(2,1)S(1)}, bf16[512,2,128]{0,2,1:T(8,128)(2,1)S(1)}, u32[]{:S(2)}, u32[]{:S(2)}) collective-permute-start(bf16[512,2,128]{0,2,1:T(8,128)(2,1)S(1)} %collective-permute-done.2), channel_id=1, source_target_pairs={{0,7},{1,0},{2,1},{3,2},{4,3},{5,4},{6,5},{7,6},{8,15},{9,8},{10,9... | collective-permute-start | bytes 786440 | tf_op jit(solution)/shard_map/ppermute | solution.py:19
  136.7 5.8 collective-permute-start.6
  138.4 10.9 %copy-start.2 = (f32[2,2,128]{2,1,0:T(2,128)S(1)}, f32[2,2,128]{2,1,0:T(2,128)}, u32[]{:S(2)}) copy-start(f32[2,2,128]{2,1,0:T(2,128)} %param.16) | copy-start | bytes 6148
  149.2 323.1 %all-gather.7.cloned.1.call-start = ((), (), s32[]{:S(2)}) async-start(), calls=%async_computation.3 | async-start | bytes 8650752 | tf_op jit(solution)/shard_map/all_gather | solution.py:30
Sparse Core Ops, SparseCore 0:
  11.2 101.4 all-gather.4
  149.4 167.5 reduce-scatter.1
  370.0 102.2 all-gather.6
